TPU v7x, 32 devices: a whole 2x2x4 slice. The times are simulated.
32 devices in a mesh: past: 4 (over y, x), second: 8 (over z, core).
Axes of the slice: x: 2, y: 2, z: 4, core: 2. Of those that a mesh axis runs over, the one named last changes fastest.
Arguments:
- resident: bfloat16 [12288, 12288], P('past', 'second'), may hold values from -6 to 6
- memory: bfloat16 [2, 384, 12288], P(None, None, 'past'), may hold values from -0.0546875 to 0.0546875
- previous: bfloat16 [2, 384, 12288], P(None, None, 'second'), may hold values from -6 to 6
- inverse_part: float32 [2, 384, 384], replicated, may hold values from -0.3125 to 0.3125
- pair_coupling: float32 [32, 32], replicated, may hold values from 0.0004510549 to 0.004510549
Outputs:
- fronts: bfloat16 [2, 384, 12288], P(None, None, 'second')
All inputs are finite; a program needn't handle non-finite values.
Results may differ from a plain program's by a relative error of at most 0.017.
Values may be sent and summed in bfloat16 or wider, within the bound.
A program may use at most 128 MiB of HBM per device.

v0:
```python
import jax
import jax.numpy as jnp
from jax import lax
from jax.sharding import PartitionSpec as P

step_size = 0.5


def orbital_flip(block, orbitals):
    row_count, col_count = block.shape
    blocks = block.reshape(row_count // orbitals, orbitals, col_count // orbitals, orbitals)
    return blocks.transpose(0, 3, 2, 1).reshape(row_count, col_count)


def solve_front(summed, prior, inverse_block):
    source = prior.astype(jnp.float32) - step_size * summed
    solved = source + jnp.dot(
        inverse_block, source, precision=lax.Precision.HIGHEST, preferred_element_type=jnp.float32
    )
    return solved.astype(jnp.bfloat16)


def self_energy(front, pair_coupling):
    orbitals = pair_coupling.shape[0]
    row_count, col_count = front.shape
    values = front.astype(jnp.float32)
    mirror = orbital_flip(values, orbitals)
    blocks = (values * values * mirror).reshape(
        row_count // orbitals, orbitals, col_count // orbitals, orbitals
    )
    return (
        (blocks * pair_coupling[None, :, None, :])
        .reshape(row_count, col_count)
        .astype(jnp.bfloat16)
    )


def per_device(resident, memory, previous, inverse_part, pair_coupling):
    past_count = lax.axis_size("past")

    def advance(memory_row, front_index):
        partial_value = jnp.dot(memory_row, resident, preferred_element_type=jnp.float32)
        summed = lax.psum(partial_value.astype(jnp.bfloat16), "past").astype(jnp.float32)
        prior_cols = previous[front_index]
        return solve_front(summed, prior_cols, inverse_part[front_index])

    front_one = advance(memory[0], 0)
    energy_one = self_energy(front_one, pair_coupling)
    band = energy_one.shape[0] // past_count
    own_rows = lax.dynamic_slice_in_dim(energy_one, lax.axis_index("past") * band, band, 0)
    wide_band = lax.all_gather(own_rows, "second", axis=1, tiled=True)
    gathered = lax.all_to_all(wide_band, "past", split_axis=1, concat_axis=0, tiled=True)
    orbitals = pair_coupling.shape[0]
    memory_next = (
        memory[1].astype(jnp.float32) + orbital_flip(gathered, orbitals).astype(jnp.float32)
    ).astype(jnp.bfloat16)
    front_two = advance(memory_next, 1)
    return jnp.stack([front_one, front_two])


def solution(mesh):
    in_specs = (P("past", "second"), P(None, None, "past"), P(None, None, "second"), P(), P())
    out_specs = P(None, None, "second")
    return jax.shard_map(
        per_device, mesh=mesh, in_specs=in_specs, out_specs=out_specs, check_vma=False
    )
```

profile of v0, /device:TPU:0, one launch (start us, length us, event | category | flops | bytes accessed | tf_op | source)
XLA Modules:
  0.0 301.7 jit_solution(1481439341360291000)
XLA Ops:
  6.5 0.0 copy-start
  6.5 0.0 all-reduce.3.cloned.1.call-start
  6.5 9.2 %convolution_convert_fusion.1 = bf16[384,1536]{1,0:T(8,128)(2,1)} fusion(bf16[3072,1536]{1,0:T(8,128)(2,1)} %param.5, bf16[2,384,3072]{2,1,0:T(8,128)(2,1)} %param.6), kind=kOutput, calls=%fused_computation.10 | convolution fusion | flops 3624468480 | bytes 12976128 | tf_op jit(solution)/shard_map/dot_general | solution.py:42
  15.8 0.0 all-reduce.3.cloned.1.call-update
  15.8 0.0 all-gather.2.cloned.1.call-start
  15.8 0.0 copy-done
  15.9 4.4 %mul.29 = f32[12,32,48,32]{3,2,1,0:T(8,128)} broadcast(f32[32,32]{1,0:T(8,128)S(1)} %copy-done), dimensions={1,3} | broadcast | bytes 2363392 | tf_op jit(solution)/shard_map/mul | solution.py:32
  20.3 6.9 %mul.30 = f32[384,1536]{1,0:T(8,128)S(1)} reshape(f32[12,32,48,32]{3,2,1,0:T(8,128)} %mul.29) | data formatting | bytes 4718592 | tf_op jit(solution)/shard_map/mul | solution.py:32
  27.2 45.8 %all-reduce.3.cloned.1.call-done = bf16[384,1536]{1,0:T(8,128)(2,1)} async-done(((bf16[384,1536]{1,0:T(8,128)(2,1)}), bf16[384,1536]{1,0:T(8,128)(2,1)}) %all-reduce.3.cloned.1.call-update) | async-done | bytes 1179664 | tf_op jit(solution)/shard_map/psum | solution.py:43
  73.0 8.3 %fusion.28 = (f32[384,1536]{1,0:T(8,128)}, bf16[384,1536]{1,0:T(8,128)(2,1)S(1)}) fusion(f32[2,384,384]{2,1,0:T(8,128)} %param.8, bf16[384,1536]{1,0:T(8,128)(2,1)} %all-reduce.3.cloned.1.call-done, bf16[2,384,1536]{2,1,0:T(8,128)(2,1)} %param.7), kind=kOutput, calls=%fused_computation.40 | convolution fusion | flops 2724397056 | bytes 8847360 | tf_op jit(solution)/shard_map/dot_general | solution.py:17
  81.3 5.0 %reshape.26 = f32[12,32,48,32]{3,2,1,0:T(8,128)} reshape(bf16[384,1536]{1,0:T(8,128)(2,1)S(1)} %get-tuple-element.6) | data formatting | bytes 3538944 | tf_op jit(solution)/shard_map/reshape | solution.py:11
  86.3 10.8 %copy.8 = f32[12,32,48,32]{3,2,1,0:T(8,128)} copy(f32[12,32,48,32]{1,2,3,0:T(8,128)} %bitcast.65) | data formatting | bytes 4718592 | tf_op jit(solution)/shard_map/transpose | solution.py:12
  97.1 7.7 %reshape.27 = f32[384,1536]{1,0:T(8,128)} reshape(f32[12,32,48,32]{3,2,1,0:T(8,128)} %copy.8) | data formatting | bytes 4718592 | tf_op jit(solution)/shard_map/reshape | solution.py:12
  104.8 2.0 fusion.21
  106.9 0.0 all-gather.2.cloned.1.call-update
  106.9 0.0 all-reduce.5.cloned.1.call-start
  106.9 31.5 %all-gather.2.cloned.1.call-done = bf16[96,12288]{1,0:T(8,128)(2,1)} async-done(((bf16[96,1536]{1,0:T(8,128)(2,1)}), bf16[96,12288]{1,0:T(8,128)(2,1)}) %all-gather.2.cloned.1.call-update) | async-done | bytes 2359312 | tf_op jit(solution)/shard_map/all_gather | solution.py:51
  138.5 1.8 copy.15
  140.3 32.0 %all_to_all.13 = bf16[96,4,3072]{2,0,1:T(8,128)(2,1)S(1)} all-to-all(bf16[96,4,3072]{2,0,1:T(8,128)(2,1)S(1)} %bitcast.66), channel_id=1, replica_groups=mesh['past'=4,'second'=8] {'past'}, dimensions={1} | all-to-all | bytes 4718592 | tf_op jit(solution)/shard_map/all_to_all | solution.py:52
  172.4 2.7 convert_bitcast_fusion
  175.1 12.3 %reshape.32 = f32[12,32,96,32]{3,2,1,0:T(8,128)} reshape(f32[4,96,3072]{2,1,0:T(8,128)} %convert_bitcast_fusion) | data formatting | bytes 9437184 | tf_op jit(solution)/shard_map/convert_element_type | solution.py:55
  187.4 22.5 %copy.10 = f32[12,32,96,32]{3,2,1,0:T(8,128)} copy(f32[12,32,96,32]{1,2,3,0:T(8,128)} %bitcast.64) | data formatting | bytes 9437184 | tf_op jit(solution)/shard_map/convert_element_type | solution.py:55
  209.9 14.6 %reshape.31 = f32[384,3072]{1,0:T(8,128)} reshape(f32[12,32,96,32]{3,2,1,0:T(8,128)} %copy.10) | data formatting | bytes 9437184 | tf_op jit(solution)/shard_map/convert_element_type | solution.py:55
  224.4 0.0 copy-start.1
  224.5 10.7 %convolution_convert_fusion = bf16[384,1536]{1,0:T(8,128)(2,1)} fusion(bf16[3072,1536]{1,0:T(8,128)(2,1)} %param.5, f32[384,3072]{1,0:T(8,128)} %reshape.31, bf16[2,384,3072]{2,1,0:T(8,128)(2,1)} %param.6), kind=kOutput, calls=%fused_computation.9 | convolution fusion | flops 3628007424 | bytes 17694720 | tf_op jit(solution)/shard_map/dot_general | solution.py:42
  235.2 0.0 all-reduce.5.cloned.1.call-update
  235.2 52.3 %all-reduce.5.cloned.1.call-done = bf16[384,1536]{1,0:T(8,128)(2,1)} async-done(((bf16[384,1536]{1,0:T(8,128)(2,1)}), bf16[384,1536]{1,0:T(8,128)(2,1)}) %all-reduce.5.cloned.1.call-update) | async-done | bytes 1179664 | tf_op jit(solution)/shard_map/psum | solution.py:43
  287.5 0.0 copy-done.1
  287.5 6.1 %fusion.5 = bf16[1,384,1536]{2,1,0:T(8,128)(2,1)S(1)} fusion(bf16[384,1536]{1,0:T(8,128)(2,1)} %all-reduce.5.cloned.1.call-done, bf16[2,384,1536]{2,1,0:T(8,128)(2,1)S(1)} %copy-done.1, f32[2,384,384]{2,1,0:T(8,128)} %param.8), kind=kOutput, calls=%fused_computation.11 | convolution fusion | flops 2723807232 | bytes 6488064 | tf_op jit(solution)/shard_map/dot_general | solution.py:17
  293.6 1.6 pad_maximum_fusion
Async XLA Ops:
  6.5 9.3 %copy-start = (f32[32,32]{1,0:T(8,128)S(1)}, f32[32,32]{1,0:T(8,128)}, u32[]{:S(2)}) copy-start(f32[32,32]{1,0:T(8,128)} %param.9) | copy-start | bytes 12292
  6.5 66.5 %all-reduce.3.cloned.1.call-start = ((), (), s32[]{:S(2)}) async-start(), calls=%async_computation.1 | async-start | bytes 2359296 | tf_op jit(solution)/shard_map/psum | solution.py:43
  15.8 122.7 %all-gather.2.cloned.1.call-start = ((), (), s32[]{:S(2)}) async-start(), calls=%async_computation.2 | async-start | bytes 2654208 | tf_op jit(solution)/shard_map/all_gather | solution.py:51
  106.9 180.6 %all-reduce.5.cloned.1.call-start = ((), (), s32[]{:S(2)}) async-start(), calls=%async_computation.3 | async-start | bytes 2359296 | tf_op jit(solution)/shard_map/psum | solution.py:43
  224.4 63.0 %copy-start.1 = (bf16[2,384,1536]{2,1,0:T(8,128)(2,1)S(1)}, bf16[2,384,1536]{2,1,0:T(8,128)(2,1)}, u32[]{:S(2)}) copy-start(bf16[2,384,1536]{2,1,0:T(8,128)(2,1)} %param.7) | copy-start | bytes 7077892
Sparse Core Ops, SparseCore 0:
  15.9 57.0 all-reduce.2
  107.0 31.4 all-gather.1
  235.3 52.1 all-reduce.4
where the time goes:
time: 303 us; the launch traced here: 302 us
  waiting for transfers between devices  130 us (43%)
  local copies, waits for them, and re-layouts  86.1 us (28%)
  matrix products  34.3 us (11%)
  blocking collectives  32 us (11%)
  between operations  13.2 us (4%)
  other arithmetic  6.39 us (2%)
    psum x2, waiting for transfers between devices, advance(): lax.psum(partial_value.astype(jnp.bfloat16), 'past').astype(jnp.float32)  98.1 us
    convert_element_type x3, local copies, waits for them, and re-layouts, per_device(): orbital_flip(gathered, orbitals).astype(jnp.float32)  49.4 us
    all_to_all x1, blocking collectives, per_device(): lax.all_to_all(wide_band, 'past', split_axis=1, concat_axis=0, tiled=True)  32 us
    all_gather x1, waiting for transfers between devices, per_device(): wide_band = lax.all_gather(own_rows, 'second', axis=1, tiled=True)  31.5 us
    dot_general x2, matrix products, advance(): jnp.dot(memory_row, resident, preferred_element_type=jnp.float32)  19.9 us
    dot_general x2, matrix products, solve_front(): jnp.dot(inverse_block, source, precision=lax.Precision.HIGHEST, preferred...  14.3 us
    mul x2, local copies, waits for them, and re-layouts, self_energy(): blocks * pair_coupling[None, :, None, :]  11.3 us
    transpose x1, local copies, waits for them, and re-layouts, orbital_flip(): return blocks.transpose(0, 3, 2, 1).reshape(row_count, col_count)  10.8 us
  transfers between devices with their start and end apart: 3, of which 3 were waited for; matrix products, arithmetic and copies ran while one was open for 4% of the time, Pallas kernels for 0%

commit v1 on v0

--- a/solution.py
+++ b/solution.py
@@ -4,6 +4,12 @@
 from jax.sharding import PartitionSpec as P
 
 step_size = 0.5
+
+
+def swap_blocks(array, name, split, join):
+    pieces = jnp.split(array, lax.axis_size(name), axis=split)
+    got = lax.all_to_all(jnp.stack(pieces), name, 0, 0)
+    return jnp.concatenate(got, axis=join)
 
 
 def orbital_flip(block, orbitals):
@@ -49,7 +55,7 @@
     band = energy_one.shape[0] // past_count
     own_rows = lax.dynamic_slice_in_dim(energy_one, lax.axis_index("past") * band, band, 0)
     wide_band = lax.all_gather(own_rows, "second", axis=1, tiled=True)
-    gathered = lax.all_to_all(wide_band, "past", split_axis=1, concat_axis=0, tiled=True)
+    gathered = swap_blocks(wide_band, "past", 1, 0)
     orbitals = pair_coupling.shape[0]
     memory_next = (
         memory[1].astype(jnp.float32) + orbital_flip(gathered, orbitals).astype(jnp.float32)

time: 303 us -> 297 us (0.980)
  local copies, waits for them, and re-layouts: 86.1 us -> 83 us
where the time goes in v1:
time: 297 us; the launch traced here: 296 us
  waiting for transfers between devices  130 us (44%)
  local copies, waits for them, and re-layouts  83 us (28%)
  matrix products  34.2 us (12%)
  blocking collectives  32 us (11%)
  between operations  13.2 us (4%)
  other arithmetic  3.95 us (1%)
    psum x2, waiting for transfers between devices, advance(): lax.psum(partial_value.astype(jnp.bfloat16), 'past').astype(jnp.float32)  98.1 us
    convert_element_type x3, local copies, waits for them, and re-layouts, per_device(): orbital_flip(gathered, orbitals).astype(jnp.float32)  46.4 us
    all_to_all x1, blocking collectives, swap_blocks(): got = lax.all_to_all(jnp.stack(pieces), name, 0, 0)  32 us
    all_gather x1, waiting for transfers between devices, per_device(): wide_band = lax.all_gather(own_rows, 'second', axis=1, tiled=True)  31.5 us
    dot_general x2, matrix products, advance(): jnp.dot(memory_row, resident, preferred_element_type=jnp.float32)  19.9 us
    dot_general x2, matrix products, solve_front(): jnp.dot(inverse_block, source, precision=lax.Precision.HIGHEST, preferred...  14.3 us
    mul x2, local copies, waits for them, and re-layouts, self_energy(): blocks * pair_coupling[None, :, None, :]  11.3 us
    transpose x1, local copies, waits for them, and re-layouts, orbital_flip(): return blocks.transpose(0, 3, 2, 1).reshape(row_count, col_count)  10.8 us
  transfers between devices with their start and end apart: 3, of which 3 were waited for; matrix products, arithmetic and copies ran while one was open for 4% of the time, Pallas kernels for 0%

profile of v1, /device:TPU:0, one launch (start us, length us, event | category | flops | bytes accessed | tf_op | source)
XLA Modules:
  0.0 296.2 jit_solution(16054703843870884580)
XLA Ops:
  6.5 0.0 copy-start
  6.5 0.0 all-reduce.3.cloned.1.call-start
  6.5 9.2 %convolution_convert_fusion.1 = bf16[384,1536]{1,0:T(8,128)(2,1)} fusion(bf16[3072,1536]{1,0:T(8,128)(2,1)} %param.5, bf16[2,384,3072]{2,1,0:T(8,128)(2,1)} %param.6), kind=kOutput, calls=%fused_computation.9 | convolution fusion | flops 3624468480 | bytes 12976128 | tf_op jit(solution)/shard_map/dot_general | solution.py:48
  15.8 0.0 all-reduce.3.cloned.1.call-update
  15.8 0.0 all-gather.2.cloned.1.call-start
  15.8 0.0 copy-done
  15.9 4.4 %mul.29 = f32[12,32,48,32]{3,2,1,0:T(8,128)} broadcast(f32[32,32]{1,0:T(8,128)S(1)} %copy-done), dimensions={1,3} | broadcast | bytes 2363392 | tf_op jit(solution)/shard_map/mul | solution.py:38
  20.3 6.9 %mul.30 = f32[384,1536]{1,0:T(8,128)S(1)} reshape(f32[12,32,48,32]{3,2,1,0:T(8,128)} %mul.29) | data formatting | bytes 4718592 | tf_op jit(solution)/shard_map/mul | solution.py:38
  27.2 45.8 %all-reduce.3.cloned.1.call-done = bf16[384,1536]{1,0:T(8,128)(2,1)} async-done(((bf16[384,1536]{1,0:T(8,128)(2,1)}), bf16[384,1536]{1,0:T(8,128)(2,1)}) %all-reduce.3.cloned.1.call-update) | async-done | bytes 1179664 | tf_op jit(solution)/shard_map/psum | solution.py:49
  73.0 8.2 %fusion.28 = (f32[384,1536]{1,0:T(8,128)}, bf16[384,1536]{1,0:T(8,128)(2,1)S(1)}) fusion(f32[2,384,384]{2,1,0:T(8,128)} %param.8, bf16[384,1536]{1,0:T(8,128)(2,1)} %all-reduce.3.cloned.1.call-done, bf16[2,384,1536]{2,1,0:T(8,128)(2,1)} %param.7), kind=kOutput, calls=%fused_computation.43 | convolution fusion | flops 2724397056 | bytes 8847360 | tf_op jit(solution)/shard_map/dot_general | solution.py:23
  81.2 5.0 %reshape.21 = f32[12,32,48,32]{3,2,1,0:T(8,128)} reshape(bf16[384,1536]{1,0:T(8,128)(2,1)S(1)} %get-tuple-element.10) | data formatting | bytes 3538944 | tf_op jit(solution)/shard_map/reshape | solution.py:17
  86.2 10.8 %copy.9 = f32[12,32,48,32]{3,2,1,0:T(8,128)} copy(f32[12,32,48,32]{1,2,3,0:T(8,128)} %bitcast.67) | data formatting | bytes 4718592 | tf_op jit(solution)/shard_map/transpose | solution.py:18
  97.0 7.7 %reshape.22 = f32[384,1536]{1,0:T(8,128)} reshape(f32[12,32,48,32]{3,2,1,0:T(8,128)} %copy.9) | data formatting | bytes 4718592 | tf_op jit(solution)/shard_map/reshape | solution.py:18
  104.8 2.0 fusion.21
  106.8 0.0 all-gather.2.cloned.1.call-update
  106.8 0.0 all-reduce.5.cloned.1.call-start
  106.9 31.5 %all-gather.2.cloned.1.call-done = bf16[96,12288]{1,0:T(8,128)(2,1)} async-done(((bf16[96,1536]{1,0:T(8,128)(2,1)}), bf16[96,12288]{1,0:T(8,128)(2,1)}) %all-gather.2.cloned.1.call-update) | async-done | bytes 2359312 | tf_op jit(solution)/shard_map/all_gather | solution.py:57
  138.4 1.8 slice_bitcast_fusion.3
  140.2 0.3 pad_maximum_fusion
  140.5 32.0 %all_to_all.5 = bf16[4,96,3072]{2,1,0:T(8,128)(2,1)S(1)} all-to-all(bf16[4,96,3072]{2,1,0:T(8,128)(2,1)S(1)} %pad_maximum_fusion), channel_id=1, replica_groups=mesh['past'=4,'second'=8] {'past'}, dimensions={0} | all-to-all | bytes 4718592 | tf_op jit(solution)/shard_map/all_to_all | solution.py:11
  172.5 9.4 %reshape.27 = f32[12,32,96,32]{3,2,1,0:T(8,128)} reshape(bf16[4,96,3072]{2,1,0:T(8,128)(2,1)S(1)} %all_to_all.5) | data formatting | bytes 7077888 | tf_op jit(solution)/shard_map/convert_element_type | solution.py:61
  181.9 22.5 %copy.10 = f32[12,32,96,32]{3,2,1,0:T(8,128)} copy(f32[12,32,96,32]{1,2,3,0:T(8,128)} %bitcast.66) | data formatting | bytes 9437184 | tf_op jit(solution)/shard_map/convert_element_type | solution.py:61
  204.4 14.6 %reshape.26 = f32[384,3072]{1,0:T(8,128)} reshape(f32[12,32,96,32]{3,2,1,0:T(8,128)} %copy.10) | data formatting | bytes 9437184 | tf_op jit(solution)/shard_map/convert_element_type | solution.py:61
  218.9 0.0 copy-start.1
  218.9 10.7 %convolution_convert_fusion = bf16[384,1536]{1,0:T(8,128)(2,1)} fusion(bf16[3072,1536]{1,0:T(8,128)(2,1)} %param.5, f32[384,3072]{1,0:T(8,128)} %reshape.26, bf16[2,384,3072]{2,1,0:T(8,128)(2,1)} %param.6), kind=kOutput, calls=%fused_computation.8 | convolution fusion | flops 3628007424 | bytes 17694720 | tf_op jit(solution)/shard_map/dot_general | solution.py:48
  229.6 0.0 all-reduce.5.cloned.1.call-update
  229.7 52.3 %all-reduce.5.cloned.1.call-done = bf16[384,1536]{1,0:T(8,128)(2,1)} async-done(((bf16[384,1536]{1,0:T(8,128)(2,1)}), bf16[384,1536]{1,0:T(8,128)(2,1)}) %all-reduce.5.cloned.1.call-update) | async-done | bytes 1179664 | tf_op jit(solution)/shard_map/psum | solution.py:49
  281.9 0.0 copy-done.1
  282.0 6.1 %fusion.5 = bf16[1,384,1536]{2,1,0:T(8,128)(2,1)S(1)} fusion(bf16[384,1536]{1,0:T(8,128)(2,1)} %all-reduce.5.cloned.1.call-done, bf16[2,384,1536]{2,1,0:T(8,128)(2,1)S(1)} %copy-done.1, f32[2,384,384]{2,1,0:T(8,128)} %param.8), kind=kOutput, calls=%fused_computation.10 | convolution fusion | flops 2723807232 | bytes 6488064 | tf_op jit(solution)/shard_map/dot_general | solution.py:23
  288.0 1.6 pad_maximum_fusion.1
Async XLA Ops:
  6.5 9.3 %copy-start = (f32[32,32]{1,0:T(8,128)S(1)}, f32[32,32]{1,0:T(8,128)}, u32[]{:S(2)}) copy-start(f32[32,32]{1,0:T(8,128)} %param.9) | copy-start | bytes 12292
  6.5 66.5 %all-reduce.3.cloned.1.call-start = ((), (), s32[]{:S(2)}) async-start(), calls=%async_computation.1 | async-start | bytes 2359296 | tf_op jit(solution)/shard_map/psum | solution.py:49
  15.8 122.6 %all-gather.2.cloned.1.call-start = ((), (), s32[]{:S(2)}) async-start(), calls=%async_computation.2 | async-start | bytes 2654208 | tf_op jit(solution)/shard_map/all_gather | solution.py:57
  106.8 175.1 %all-reduce.5.cloned.1.call-start = ((), (), s32[]{:S(2)}) async-start(), calls=%async_computation.3 | async-start | bytes 2359296 | tf_op jit(solution)/shard_map/psum | solution.py:49
  218.9 63.0 %copy-start.1 = (bf16[2,384,1536]{2,1,0:T(8,128)(2,1)S(1)}, bf16[2,384,1536]{2,1,0:T(8,128)(2,1)}, u32[]{:S(2)}) copy-start(bf16[2,384,1536]{2,1,0:T(8,128)(2,1)} %param.7) | copy-start | bytes 7077892
Sparse Core Ops, SparseCore 0:
  15.9 57.0 all-reduce.2
  106.9 31.4 all-gather.1
  229.8 52.1 all-reduce.4
